TPU v7x, 32 devices: a whole 2x2x4 slice. The times are simulated.
32 devices in a mesh: groups: 2 (over y), tensor: 4 (over z), dp: 4 (over x, core).
Axes of the slice: x: 2, y: 2, z: 4, core: 2. Of those that a mesh axis runs over, the one named last changes fastest.
Arguments:
- out_grad: bfloat16 [4, 1280, 4096], P('dp', ('groups', 'tensor')), parts along dimension 1, may hold values from -6 to 6
- gate_pre: bfloat16 [4, 1280, 14336], P('dp', 'groups', 'tensor'), parts along dimension 1, may hold values from -8 to 8
- up_pre: bfloat16 [4, 1280, 14336], P('dp', 'groups', 'tensor'), parts along dimension 1, may hold values from -6 to 6
- down_weight: bfloat16 [14336, 4096], P('tensor'), may hold values from -0.046875 to 0.046875
Outputs:
- gate_grad: bfloat16 [4, 1280, 14336], P('dp', 'groups', 'tensor'), parts along dimension 1
- up_grad: bfloat16 [4, 1280, 14336], P('dp', 'groups', 'tensor'), parts along dimension 1
- down_grad: bfloat16 [28672, 4096], P(('groups', 'tensor'), 'dp'), parts along dimension 0
There are 2 independent parts, one for each index of `groups`. A program takes and returns all parts, laid end to end along the dimension named above; an argument that names none is the same for every part. Nothing has to cross between parts.
All inputs are finite; a program needn't handle non-finite values.
Results may differ from a plain program's by a relative error of at most 0.014.
Values may be sent and summed in bfloat16 or wider, within the bound.
A program may use at most 128 MiB of HBM per device.

v0:
```python
import math
import jax
import jax.numpy as jnp
from jax import lax
from jax.sharding import PartitionSpec as P


def on_device(out_grad, gate_pre, up_pre, down_weight):
    gate = gate_pre[0].astype(jnp.float32)
    up = up_pre[0].astype(jnp.float32)
    sig = jax.nn.sigmoid(gate)
    act = gate * sig
    hidden = (act * up).astype(jnp.bfloat16)
    scale = 1.0 / math.sqrt(hidden.shape[0] * lax.axis_size("dp"))
    hidden_all = lax.all_gather(hidden, "dp", axis=0, tiled=True)
    block = lax.all_gather(out_grad, "tensor", axis=1, tiled=True)[0]
    columns = lax.all_to_all(block, "dp", split_axis=1, concat_axis=0, tiled=True)
    hidden_grad = lax.dot_general(
        block, down_weight, (((1,), (1,)), ((), ())), preferred_element_type=jnp.float32
    )
    gate_grad = (hidden_grad * up * sig * (1.0 + gate * (1.0 - sig))).astype(jnp.bfloat16)
    up_grad = (hidden_grad * act).astype(jnp.bfloat16)
    total = jnp.einsum("tf,td->fd", hidden_all, columns, preferred_element_type=jnp.float32)
    down_grad = (total * scale).astype(jnp.bfloat16)
    return (gate_grad[None], up_grad[None], down_grad)


def solution(mesh):
    return jax.shard_map(
        on_device,
        mesh=mesh,
        in_specs=(
            P("dp", ("groups", "tensor"), None),
            P("dp", "groups", "tensor"),
            P("dp", "groups", "tensor"),
            P("tensor", None),
        ),
        out_specs=(
            P("dp", "groups", "tensor"),
            P("dp", "groups", "tensor"),
            P(("groups", "tensor"), "dp"),
        ),
        check_vma=False,
    )
```

profile of v0, /device:TPU:0, one launch (start us, length us, event | category | flops | bytes accessed | tf_op | source)
XLA Modules:
  0.0 347.5 jit_solution(11023457217963688195)
XLA Ops:
  7.2 0.0 all-gather.3.cloned.1.call-start
  7.2 0.7 all-gather.3.cloned.1.call-update
  7.9 0.0 all-gather.5.cloned.1.call-start
  7.9 102.4 %all-gather.3.cloned.1.call-done = bf16[1,640,4096]{2,1,0:T(8,128)(2,1)} async-done(((bf16[1,160,4096]{2,1,0:T(8,128)(2,1)}), bf16[1,640,4096]{2,1,0:T(8,128)(2,1)}) %all-gather.3.cloned.1.call-update) | async-done | bytes 5242896 | tf_op jit(solution)/shard_map/all_gather | solution.py:16
  110.4 33.4 %fusion.10 = (bf16[1,640,3584]{2,1,0:T(8,128)(2,1)}, bf16[1,640,3584]{2,1,0:T(8,128)(2,1)}, bf16[640,3584]{1,0:T(8,128)(2,1)}) fusion(bf16[1,640,3584]{2,1,0:T(8,128)(2,1)} %param.5, bf16[1,640,3584]{2,1,0:T(8,128)(2,1)} %param.6, bf16[3584,4096]{1,0:T(8,128)(2,1)} %param.7, bf16[1,640,4096]{2,1,0:T(8,128)(2,1)} %all-gather.3.cloned.1.call-done), kind=kOutput, calls=%fused_computation.17 | convolution fusion | flops 18829475840 | bytes 57540608 | tf_op jit(solution)/shard_map/dot_general | solution.py:18
  143.8 0.0 all-gather.5.cloned.1.call-update
  143.8 8.1 %copy.9 = bf16[1,640,4096]{1,2,0:T(8,128)(2,1)} copy(bf16[1,640,4096]{2,1,0:T(8,128)(2,1)} %all-gather.3.cloned.1.call-done) | data formatting | bytes 10485760 | tf_op jit(solution)/shard_map/all_gather | solution.py:16
  151.9 122.0 %all_to_all.19 = bf16[640,4,1024]{0,2,1:T(8,128)(2,1)} all-to-all(bf16[640,4,1024]{0,2,1:T(8,128)(2,1)} %bitcast.31), channel_id=1, replica_groups=mesh['groups'=2,'tensor'=4,'dp'=4] {'dp'}, dimensions={1} | all-to-all | bytes 10485760 | tf_op jit(solution)/shard_map/all_to_all | solution.py:17
  274.0 8.0 %copy.10 = bf16[4,640,1024]{2,1,0:T(8,128)(2,1)} copy(bf16[4,640,1024]{1,2,0:T(8,128)(2,1)} %bitcast.32) | data formatting | bytes 10485760 | tf_op jit(solution)/shard_map/all_to_all | solution.py:17
  282.0 33.6 %all-gather.5.cloned.1.call-done = bf16[2560,3584]{1,0:T(8,128)(2,1)} async-done(((bf16[640,3584]{1,0:T(8,128)(2,1)}), bf16[2560,3584]{1,0:T(8,128)(2,1)}) %all-gather.5.cloned.1.call-update) | async-done | bytes 18350096 | tf_op jit(solution)/shard_map/all_gather | solution.py:15
  315.6 25.0 %multiply_convert_fusion = bf16[3584,1024]{1,0:T(8,128)(2,1)} fusion(bf16[2560,3584]{1,0:T(8,128)(2,1)} %all-gather.5.cloned.1.call-done, bf16[2560,1024]{1,0:T(8,128)(2,1)} %bitcast.33), kind=kOutput, calls=%fused_computation | convolution fusion | flops 18797821952 | bytes 30932992 | tf_op jit(solution)/shard_map/tf,td->fd/dot_general | solution.py:23
Async XLA Ops:
  7.2 103.2 %all-gather.3.cloned.1.call-start = ((), (), s32[]{:S(2)}) async-start(), calls=%async_computation.1 | async-start | bytes 6553600 | tf_op jit(solution)/shard_map/all_gather | solution.py:16
  7.9 307.7 %all-gather.5.cloned.1.call-start = ((), (), s32[]{:S(2)}) async-start(), calls=%async_computation.2 | async-start | bytes 22937600 | tf_op jit(solution)/shard_map/all_gather | solution.py:15
Sparse Core Ops, SparseCore 0:
  9.6 100.7 all-gather.2
  143.9 171.6 all-gather.4
where the time goes:
time: 348 us; the launch traced here: 347 us
  waiting for transfers between devices  137 us (39%)
  blocking collectives  122 us (35%)
  matrix products  58.4 us (17%)
  local copies, waits for them, and re-layouts  16.2 us (5%)
  between operations  14 us (4%)
    all_to_all x1, blocking collectives, on_device(): lax.all_to_all(block, 'dp', split_axis=1, concat_axis=0, tiled=True)  122 us
    all_gather x1, waiting for transfers between devices, on_device(): block = lax.all_gather(out_grad, 'tensor', axis=1, tiled=True)[0]  102 us
    all_gather x1, waiting for transfers between devices, on_device(): hidden_all = lax.all_gather(hidden, 'dp', axis=0, tiled=True)  33.6 us
    dot_general x1, matrix products, on_device(): lax.dot_general(block, down_weight, (((1,), (1,)), ((), ())), preferred_e...  33.4 us
    dot_general x1, matrix products, on_device(): jnp.einsum('tf,td->fd', hidden_all, columns, preferred_element_type=jnp.f...  25 us
    all_gather x1, local copies, waits for them, and re-layouts, on_device(): block = lax.all_gather(out_grad, 'tensor', axis=1, tiled=True)[0]  8.13 us
    all_to_all x1, local copies, waits for them, and re-layouts, on_device(): lax.all_to_all(block, 'dp', split_axis=1, concat_axis=0, tiled=True)  8.05 us
  transfers between devices with their start and end apart: 2, of which 2 were waited for; matrix products, arithmetic and copies ran while one was open for 5% of the time, Pallas kernels for 0%

commit v1 on v0

--- a/solution.py
+++ b/solution.py
@@ -3,6 +3,22 @@
 import jax.numpy as jnp
 from jax import lax
 from jax.sharding import PartitionSpec as P
+from jax.lax import axis_index, axis_size, ppermute
+
+
+def _deliver_fields(frame_in, link_axis, work_x):
+    piece_out = axis_size(link_axis)
+    everything, raw_out, piece_next = (piece_out, axis_index(link_axis), frame_in.shape[0])
+    buffers = []
+    for ii in range(everything):
+        buffers.append((ii, (ii + 1) % everything))
+    work_now, local_out = (frame_in, None)
+    for nth in range(everything):
+        s_next = ppermute(work_now, link_axis, buffers) if nth < everything - 1 else None
+        res = work_x(work_now, (raw_out - nth) % everything * piece_next)
+        local_out = res if local_out is None else local_out + res
+        work_now = s_next
+    return local_out
 
 
 def on_device(out_grad, gate_pre, up_pre, down_weight):
@@ -12,7 +28,6 @@
     act = gate * sig
     hidden = (act * up).astype(jnp.bfloat16)
     scale = 1.0 / math.sqrt(hidden.shape[0] * lax.axis_size("dp"))
-    hidden_all = lax.all_gather(hidden, "dp", axis=0, tiled=True)
     block = lax.all_gather(out_grad, "tensor", axis=1, tiled=True)[0]
     columns = lax.all_to_all(block, "dp", split_axis=1, concat_axis=0, tiled=True)
     hidden_grad = lax.dot_general(
@@ -20,7 +35,16 @@
     )
     gate_grad = (hidden_grad * up * sig * (1.0 + gate * (1.0 - sig))).astype(jnp.bfloat16)
     up_grad = (hidden_grad * act).astype(jnp.bfloat16)
-    total = jnp.einsum("tf,td->fd", hidden_all, columns, preferred_element_type=jnp.float32)
+    total = _deliver_fields(
+        hidden,
+        "dp",
+        lambda part, offset: jnp.einsum(
+            "tf,td->fd",
+            part,
+            lax.dynamic_slice_in_dim(columns, offset, part.shape[0], axis=0),
+            preferred_element_type=jnp.float32,
+        ),
+    )
     down_grad = (total * scale).astype(jnp.bfloat16)
     return (gate_grad[None], up_grad[None], down_grad)
 

time: 348 us -> 384 us (1.10)
  blocking collectives: 122 us -> 0 us
  waiting for transfers between devices: 137 us -> 258 us
  matrix products: 58.4 us -> 88.3 us
  starting transfers between devices: 0.08 us -> 5.12 us
    ppermute x0 -> x3, waiting for transfers between devices: none -> 141 us  [_deliver_fields(): ppermute(work_now, link_axis, buffers)]
    all_to_all x1 -> x0, blocking collectives: 122 us -> none  [on_device(): lax.all_to_all(block, 'dp', split_axis=1, concat_axis=0, tiled=True)]
    all_gather x1 -> x0, waiting for transfers between devices: 33.6 us -> none  [on_device(): hidden_all = lax.all_gather(hidden, 'dp', axis=0, tiled=True)]
    dot_general x1 -> x4, matrix products: 25 us -> 55.3 us  [on_device(): jnp.einsum('tf,td->fd', part, lax.dynamic_slice_in_dim(columns, offset, p...]
    all_to_all x0 -> x1, waiting for transfers between devices: none -> 14 us  [on_device(): lax.all_to_all(block, 'dp', split_axis=1, concat_axis=0, tiled=True)]
    all_to_all x0 -> x1, starting transfers between devices: none -> 5.07 us  [on_device(): lax.all_to_all(block, 'dp', split_axis=1, concat_axis=0, tiled=True)]
  transfers between devices with their start and end apart: 2 -> 5, of which waited for: 2 -> 5; matrix products, arithmetic and copies ran while one was open for 5% -> 13% of each run, Pallas kernels for 0% -> 0%
where the time goes in v1:
time: 384 us; the launch traced here: 383 us
  waiting for transfers between devices  258 us (67%)
  matrix products  88.3 us (23%)
  local copies, waits for them, and re-layouts  17.9 us (5%)
  between operations  14 us (4%)
  starting transfers between devices  5.12 us (1%)
    ppermute x3, waiting for transfers between devices, _deliver_fields(): ppermute(work_now, link_axis, buffers)  141 us
    all_gather x1, waiting for transfers between devices, on_device(): block = lax.all_gather(out_grad, 'tensor', axis=1, tiled=True)[0]  102 us
    dot_general x4, matrix products, on_device(): jnp.einsum('tf,td->fd', part, lax.dynamic_slice_in_dim(columns, offset, p...  55.3 us
    dot_general x1, matrix products, on_device(): lax.dot_general(block, down_weight, (((1,), (1,)), ((), ())), preferred_e...  33 us
    all_to_all x1, waiting for transfers between devices, on_device(): lax.all_to_all(block, 'dp', split_axis=1, concat_axis=0, tiled=True)  14 us
    all_to_all x1, local copies, waits for them, and re-layouts, on_device(): lax.all_to_all(block, 'dp', split_axis=1, concat_axis=0, tiled=True)  7.85 us
    all_gather x1, local copies, waits for them, and re-layouts, on_device(): block = lax.all_gather(out_grad, 'tensor', axis=1, tiled=True)[0]  7.84 us
  transfers between devices with their start and end apart: 5, of which 5 were waited for; matrix products, arithmetic and copies ran while one was open for 13% of the time, Pallas kernels for 0%

profile of v1, /device:TPU:0, one launch (start us, length us, event | category | flops | bytes accessed | tf_op | source)
XLA Modules:
  0.0 383.1 jit_solution(3805921569988964307)
XLA Ops:
  7.2 0.0 all-gather.2.cloned.1.call-start
  7.2 0.7 all-gather.2.cloned.1.call-update
  7.9 102.5 %all-gather.2.cloned.1.call-done = bf16[1,640,4096]{2,1,0:T(8,128)(2,1)} async-done(((bf16[1,160,4096]{2,1,0:T(8,128)(2,1)}), bf16[1,640,4096]{2,1,0:T(8,128)(2,1)}) %all-gather.2.cloned.1.call-update) | async-done | bytes 5242896 | tf_op jit(solution)/shard_map/all_gather | solution.py:31
  110.4 33.0 %fusion.10 = (bf16[1,640,3584]{2,1,0:T(8,128)(2,1)}, bf16[1,640,3584]{2,1,0:T(8,128)(2,1)}, bf16[640,3584]{1,0:T(8,128)(2,1)S(1)}) fusion(bf16[1,640,3584]{2,1,0:T(8,128)(2,1)} %param.5, bf16[1,640,3584]{2,1,0:T(8,128)(2,1)} %param.6, bf16[3584,4096]{1,0:T(8,128)(2,1)} %param.7, bf16[1,640,4096]{2,1,0:T(8,128)(2,1)} %all-gather.2.cloned.1.call-done), kind=kOutput, calls=%fused_computation.17 | convolution fusion | flops 18829475840 | bytes 57540608 | tf_op jit(solution)/shard_map/dot_general | solution.py:33
  143.3 0.0 copy-start.1
  143.3 2.2 copy-done.1
  145.5 0.0 collective-permute-start
  145.5 52.2 %collective-permute-done = bf16[640,3584]{1,0:T(8,128)(2,1)} collective-permute-done((bf16[640,3584]{1,0:T(8,128)(2,1)S(1)}, bf16[640,3584]{1,0:T(8,128)(2,1)}, u32[]{:S(2)}, u32[]{:S(2)}) %collective-permute-start) | collective-permute-done | bytes 4587552 | tf_op jit(solution)/shard_map/ppermute | solution.py:17
  197.8 0.0 collective-permute-start.1
  197.8 7.8 %copy.9 = bf16[1,640,4096]{1,2,0:T(8,128)(2,1)} copy(bf16[1,640,4096]{2,1,0:T(8,128)(2,1)} %all-gather.2.cloned.1.call-done) | data formatting | bytes 10485760 | tf_op jit(solution)/shard_map/all_gather | solution.py:31
  205.6 5.1 %all-to-all-start = ((bf16[640,4,1024]{0,2,1:T(8,128)(2,1)}), bf16[640,4,1024]{0,2,1:T(8,128)(2,1)}, u32[]{:S(2)}, u32[]{:S(2)}) async-start(bf16[640,4,1024]{0,2,1:T(8,128)(2,1)} %bitcast.33), calls=%async_computation | async-start | bytes 10485760 | tf_op jit(solution)/shard_map/all_to_all | solution.py:32
  210.7 67.6 %collective-permute-done.1 = bf16[640,3584]{1,0:T(8,128)(2,1)} collective-permute-done((bf16[640,3584]{1,0:T(8,128)(2,1)}, bf16[640,3584]{1,0:T(8,128)(2,1)}, u32[]{:S(2)}, u32[]{:S(2)}) %collective-permute-start.1) | collective-permute-done | bytes 4587552 | tf_op jit(solution)/shard_map/ppermute | solution.py:17
  278.3 0.0 collective-permute-start.2
  278.3 14.0 %all-to-all-done = bf16[640,4,1024]{0,2,1:T(8,128)(2,1)} async-done(((bf16[640,4,1024]{0,2,1:T(8,128)(2,1)}), bf16[640,4,1024]{0,2,1:T(8,128)(2,1)}, u32[]{:S(2)}, u32[]{:S(2)}) %all-to-all-start) | async-done | bytes 5242912 | tf_op jit(solution)/shard_map/all_to_all | solution.py:32
  292.4 7.9 %copy.10 = bf16[4,640,1024]{2,1,0:T(8,128)(2,1)} copy(bf16[4,640,1024]{1,2,0:T(8,128)(2,1)} %bitcast.8) | data formatting | bytes 10485760 | tf_op jit(solution)/shard_map/all_to_all | solution.py:32
  300.2 0.0 copy-start
  300.2 11.8 %fusion.17 = f32[3584,1024]{1,0:T(8,128)} fusion(bf16[640,3584]{1,0:T(8,128)(2,1)} %copy-done.1, bf16[2560,1024]{1,0:T(8,128)(2,1)} %bitcast.34, s32[]{:T(128)S(6)} %select_n.32), kind=kOutput, calls=%fused_computation.24 | convolution fusion | flops 4697620480 | bytes 20578308 | tf_op jit(solution)/shard_map/tf,td->fd/dot_general | solution.py:41
  312.0 0.0 copy-done
  312.0 11.4 %fusion.15 = f32[3584,1024]{1,0:T(8,128)} fusion(bf16[640,3584]{1,0:T(8,128)(2,1)} %collective-permute-done, bf16[2560,1024]{1,0:T(8,128)(2,1)S(1)} %bitcast.35, s32[]{:T(128)S(6)} %select_n.34), kind=kOutput, calls=%fused_computation.22 | convolution fusion | flops 4697620480 | bytes 20578308 | tf_op jit(solution)/shard_map/tf,td->fd/dot_general | solution.py:41
  323.4 11.5 %fusion.13 = f32[3584,1024]{1,0:T(8,128)} fusion(bf16[640,3584]{1,0:T(8,128)(2,1)} %collective-permute-done.1, bf16[2560,1024]{1,0:T(8,128)(2,1)S(1)} %bitcast.36, s32[]{:T(128)S(6)} %select_n.36), kind=kOutput, calls=%fused_computation.20 | convolution fusion | flops 4697620480 | bytes 20578308 | tf_op jit(solution)/shard_map/tf,td->fd/dot_general | solution.py:41
  334.9 20.7 %collective-permute-done.2 = bf16[640,3584]{1,0:T(8,128)(2,1)} collective-permute-done((bf16[640,3584]{1,0:T(8,128)(2,1)}, bf16[640,3584]{1,0:T(8,128)(2,1)}, u32[]{:S(2)}, u32[]{:S(2)}) %collective-permute-start.2) | collective-permute-done | bytes 4587552 | tf_op jit(solution)/shard_map/ppermute | solution.py:17
  355.6 20.7 %multiply_convert_fusion = bf16[3584,1024]{1,0:T(8,128)(2,1)} fusion(f32[3584,1024]{1,0:T(8,128)} %fusion.13, f32[3584,1024]{1,0:T(8,128)} %fusion.17, f32[3584,1024]{1,0:T(8,128)} %fusion.15, bf16[640,3584]{1,0:T(8,128)(2,1)} %collective-permute-done.2, bf16[2560,1024]{1,0:T(8,128)(2,1)S(1)} %bitcast.37, s32[]{:T(128)S(6)} %select_n.38), kind=kOutput, calls=%fused_computation | convolution fusion | flops 4715970560 | bytes 57278468 | tf_op jit(solution)/shard_map/tf,td->fd/dot_general | solution.py:41
Async XLA Ops:
  7.2 103.2 %all-gather.2.cloned.1.call-start = ((), (), s32[]{:S(2)}) async-start(), calls=%async_computation.1 | async-start | bytes 6553600 | tf_op jit(solution)/shard_map/all_gather | solution.py:31
  143.3 2.2 copy-start.1
  145.5 52.2 %collective-permute-start = (bf16[640,3584]{1,0:T(8,128)(2,1)S(1)}, bf16[640,3584]{1,0:T(8,128)(2,1)}, u32[]{:S(2)}, u32[]{:S(2)}) collective-permute-start(bf16[640,3584]{1,0:T(8,128)(2,1)S(1)} %get-tuple-element.5), channel_id=1, source_target_pairs={{0,1},{1,2},{2,3},{3,0},{4,5},{5,6},{6,7},{7,4},{8,9},{9,10},{10,1... | collective-permute-start | bytes 13762568 | tf_op jit(solution)/shard_map/ppermute | solution.py:17
  197.8 80.5 %collective-permute-start.1 = (bf16[640,3584]{1,0:T(8,128)(2,1)}, bf16[640,3584]{1,0:T(8,128)(2,1)}, u32[]{:S(2)}, u32[]{:S(2)}) collective-permute-start(bf16[640,3584]{1,0:T(8,128)(2,1)} %collective-permute-done), channel_id=1, source_target_pairs={{0,1},{1,2},{2,3},{3,0},{4,5},{5,6},{6,7},{7,4},{8,9},{9,10},{10,1... | collective-permute-start | bytes 13762568 | tf_op jit(solution)/shard_map/ppermute | solution.py:17
  205.6 86.8 %all-to-all-start = ((bf16[640,4,1024]{0,2,1:T(8,128)(2,1)}), bf16[640,4,1024]{0,2,1:T(8,128)(2,1)}, u32[]{:S(2)}, u32[]{:S(2)}) async-start(bf16[640,4,1024]{0,2,1:T(8,128)(2,1)} %bitcast.33), calls=%async_computation | async-start | bytes 10485760 | tf_op jit(solution)/shard_map/all_to_all | solution.py:32
  278.3 77.2 %collective-permute-start.2 = (bf16[640,3584]{1,0:T(8,128)(2,1)}, bf16[640,3584]{1,0:T(8,128)(2,1)}, u32[]{:S(2)}, u32[]{:S(2)}) collective-permute-start(bf16[640,3584]{1,0:T(8,128)(2,1)} %collective-permute-done.1), channel_id=1, source_target_pairs={{0,1},{1,2},{2,3},{3,0},{4,5},{5,6},{6,7},{7,4},{8,9},{9,10},{10,1... | collective-permute-start | bytes 13762568 | tf_op jit(solution)/shard_map/ppermute | solution.py:17
  300.2 11.8 %copy-start = (bf16[4,640,1024]{2,1,0:T(8,128)(2,1)S(1)}, bf16[4,640,1024]{2,1,0:T(8,128)(2,1)}, u32[]{:S(2)}) copy-start(bf16[4,640,1024]{2,1,0:T(8,128)(2,1)} %copy.10) | copy-start | bytes 15728644
Sparse Core Ops, SparseCore 0:
  9.6 100.7 all-gather.1
